TPU v7x, 32 devices: a whole 2x2x4 slice. The times are simulated.
32 devices in a mesh: cam: 4 (over x, core), pt: 8 (over z, y).
Axes of the slice: x: 2, y: 2, z: 4, core: 2. Of those that a mesh axis runs over, the one named last changes fastest.
Arguments:
- right_side: float32 [9, 65536], P(None, ('cam', 'pt')), may hold values from -6 to 6
- cam_damping: float32 [9, 65536], P(None, ('cam', 'pt')), may hold values from 0.5 to 4
- point_damping: float32 [524288], P('pt'), may hold values from 0.1 to 1
- block_ids: int32 [4, 8, 64], P('cam', 'pt'), may hold values from 0 to 255, as said below
- slab_ids: int32 [4, 8, 64], P('cam', 'pt'), may hold values from 0 to 15
- cam_index: int32 [4, 8, 64, 4096], P('cam', 'pt'), may hold values from 0 to 63
- cam_jacobian: bfloat16 [4, 8, 64, 18, 4096], P('cam', 'pt'), may hold values from -0.59765625 to 0.59765625
- point_jacobian: bfloat16 [4, 8, 64, 6, 4096], P('cam', 'pt'), may hold values from -1.796875 to 1.796875
- pair_count: int32 [4, 8], P('cam', 'pt'), may hold values from 16 to 64, as said below
Outputs:
- solution: float32 [9, 65536], P(None, ('cam', 'pt'))
- residual: float32 [9, 65536], P(None, ('cam', 'pt'))
Inputs may be any that keep to these rules, and one draw needn't show every extreme that they name: pair_count is 64 divided by a whole number from 1 to 4, rounded down; at least one device has all 64 slots used in every draw. The owner of a block is block_ids // 32; in every device's list at most 16 slots name blocks of one owner, and in every list some owner is named by exactly 16 slots.
All inputs are finite; a program needn't handle non-finite values.
Results may differ from a plain program's by a relative error of at most 0.0003.
Values sent between devices are 32-bit elements; how exact they have to be, the bound alone decides.
A program may use at most 128 MiB of HBM per device.

v0:
```python
import jax
import jax.numpy as jnp
from jax import lax
from jax.sharding import PartitionSpec as P

BLOCK = 64
ITERS = 2
HIGH = lax.Precision.HIGHEST


def hessian_terms(pt_jac):
    combos = [(0, 0), (0, 1), (0, 2), (1, 1), (1, 2), (2, 2)]
    return jnp.stack(
        [
            jnp.sum(pt_jac[:, :, first].astype(jnp.float32) * pt_jac[:, :, second], axis=1)
            for first, second in combos
        ],
        axis=1,
    )


def collect(selector, terms):
    summed = jnp.einsum("ps,pkn->ksn", selector, terms, precision=HIGH)
    return summed.reshape(terms.shape[1], -1)


def invert_points(hess, damping):
    entry_xx = hess[0] + damping
    entry_xy = hess[1]
    entry_xz = hess[2]
    entry_yy = hess[3] + damping
    entry_yz = hess[4]
    entry_zz = hess[5] + damping
    cof_xx = entry_yy * entry_zz - entry_yz * entry_yz
    cof_xy = entry_xz * entry_yz - entry_xy * entry_zz
    cof_xz = entry_xy * entry_yz - entry_xz * entry_yy
    cof_yy = entry_xx * entry_zz - entry_xz * entry_xz
    cof_yz = entry_xy * entry_xz - entry_xx * entry_yz
    cof_zz = entry_xx * entry_yy - entry_xy * entry_xy
    determinant = entry_xx * cof_xx + entry_xy * cof_xy + entry_xz * cof_xz
    return jnp.stack([cof_xx, cof_xy, cof_xz, cof_yy, cof_yz, cof_zz]) / determinant


def apply_inverse(inverse, vector):
    out_x = inverse[0] * vector[0] + inverse[1] * vector[1] + inverse[2] * vector[2]
    out_y = inverse[1] * vector[0] + inverse[3] * vector[1] + inverse[4] * vector[2]
    out_z = inverse[2] * vector[0] + inverse[4] * vector[1] + inverse[5] * vector[2]
    return jnp.stack([out_x, out_y, out_z])


def select_cameras(picked, index_here):
    pairs = picked.shape[0]

    def select_per_group(pieces):
        picked_group, index_group = pieces
        one_hot = (
            index_group[:, :, None] == jnp.arange(BLOCK, dtype=jnp.int32)[None, None, :]
        ).astype(jnp.float32)
        return jnp.einsum("gkb,gnb->gkn", picked_group, one_hot, precision=HIGH)

    grouped = lax.map(
        select_per_group,
        (picked.reshape(pairs // 8, 8, 9, BLOCK), index_here.reshape(pairs // 8, 8, -1)),
    )
    return grouped.reshape(pairs, 9, -1)


def project(cam_panel, blocks_here, index_here, cam_jac):
    grouped = cam_panel.reshape(9, -1, BLOCK).transpose(1, 0, 2)
    picked = grouped[blocks_here]
    at_camera = select_cameras(picked, index_here)
    return jnp.sum(cam_jac * at_camera[:, None], axis=2)


def camera_sums(pushed, index_here):
    pairs = pushed.shape[0]

    def camera_per_group(pieces):
        pushed_group, index_group = pieces
        one_hot = (
            index_group[:, :, None] == jnp.arange(BLOCK, dtype=jnp.int32)[None, None, :]
        ).astype(jnp.float32)
        return jnp.einsum("gkn,gnb->gkb", pushed_group, one_hot, precision=HIGH)

    grouped = lax.map(
        camera_per_group,
        (pushed.reshape(pairs // 8, 8, 9, -1), index_here.reshape(pairs // 8, 8, -1)),
    )
    return grouped.reshape(pairs, 9, BLOCK)


def dot_whole(first, second):
    return lax.psum(jnp.sum(first * second), "cam")


def per_device(
    right_side,
    cam_damping,
    point_damping,
    block_ids,
    slab_ids,
    cam_index,
    cam_jacobian,
    point_jacobian,
    pair_count,
):
    pairs = block_ids.shape[2]
    slab_len = cam_index.shape[3]
    slabs = point_damping.shape[0] // slab_len
    cam_dev = right_side.shape[1]
    owners_count = lax.axis_size("pt")
    blk_owner = cam_dev // BLOCK
    blk_group = blk_owner * owners_count
    blocks_here = block_ids.reshape(pairs)
    slabs_here = slab_ids.reshape(pairs)
    index_here = cam_index.reshape(pairs, slab_len)
    cam_jac = cam_jacobian.reshape(pairs, 2, 9, slab_len)
    pt_jac = point_jacobian.reshape(pairs, 2, 3, slab_len)
    live_pairs = (jnp.arange(pairs, dtype=jnp.int32) < pair_count.reshape(())).astype(jnp.float32)
    slab_onehot = (slabs_here[:, None] == jnp.arange(slabs, dtype=jnp.int32)[None, :]).astype(
        jnp.float32
    )
    selector = slab_onehot * live_pairs[:, None]
    block_onehot = (blocks_here[:, None] == jnp.arange(blk_group, dtype=jnp.int32)[None, :]).astype(
        jnp.float32
    )
    hess_local = collect(selector, hessian_terms(pt_jac))
    inverse = invert_points(lax.psum(hess_local, "cam"), point_damping)
    residual, damping_here = (
        lax.all_gather(right_side, "pt", axis=1, tiled=True),
        lax.all_gather(cam_damping, "pt", axis=1, tiled=True),
    )
    solution = jnp.zeros_like(residual)
    direction = residual
    norm_now = dot_whole(residual, residual)
    for iteration in range(ITERS):
        projected = project(direction, blocks_here, index_here, cam_jac)
        pulled = jnp.sum(pt_jac * projected[:, :, None], axis=1)
        eliminated = apply_inverse(inverse, lax.psum(collect(selector, pulled), "cam")).reshape(
            3, slabs, slab_len
        )
        pulled_back = jnp.einsum("ps,ksn->pkn", slab_onehot, eliminated, precision=HIGH)
        miss = projected - jnp.sum(pt_jac * pulled_back[:, None], axis=2)
        pushed = jnp.sum(cam_jac * miss[:, :, None], axis=1)
        group_sum = jnp.einsum(
            "pg,pkb->kgb",
            block_onehot,
            camera_sums(pushed, index_here) * live_pairs[:, None, None],
            precision=HIGH,
        )
        image = damping_here * direction + lax.psum(group_sum.reshape(9, blk_group * BLOCK), "pt")
        step_size = norm_now / dot_whole(direction, image)
        solution = solution + step_size * direction
        residual = residual - step_size * image
        norm_next = dot_whole(residual, residual)
        direction = residual + norm_next / norm_now * direction
        norm_now = norm_next
    start = lax.axis_index("pt") * cam_dev
    solution = lax.dynamic_slice_in_dim(solution, start, cam_dev, 1)
    residual = lax.dynamic_slice_in_dim(residual, start, cam_dev, 1)
    return (solution, residual)


def solution(mesh):
    in_specs = (
        P(None, ("cam", "pt")),
        P(None, ("cam", "pt")),
        P("pt"),
        P("cam", "pt", None),
        P("cam", "pt", None),
        P("cam", "pt", None, None),
        P("cam", "pt", None, None, None),
        P("cam", "pt", None, None, None),
        P("cam", "pt"),
    )
    out_specs = (P(None, ("cam", "pt")), P(None, ("cam", "pt")))
    return jax.shard_map(
        per_device, mesh=mesh, in_specs=in_specs, out_specs=out_specs, check_vma=False
    )
```

profile of v0, /device:TPU:0, one launch (start us, length us, event | category | flops | bytes accessed | tf_op | source)
XLA Modules:
  0.0 737.0 jit_solution(18072257541709590716)
XLA Ops:
  18.2 34.7 %all_gather.6 = f32[9,16384]{1,0:T(8,128)S(1)} all-gather(f32[9,2048]{1,0:T(8,128)S(1)} %copy-done.11), channel_id=1, replica_groups=mesh['cam'=4,'pt'=8] {'pt'}, dimensions={1}, use_global_device_ids=true | all-gather | bytes 663552 | tf_op jit(solution)/shard_map/all_gather | solution.py:130
  57.7 7.8 %broadcast.107.clone = f32[8,8,9,4096]{3,2,1,0:T(8,128)} broadcast(f32[]{:T(128)} %constant.49.clone.1), dimensions={} | broadcast | bytes 9437188 | tf_op jit(solution)/shard_map/broadcast.5
  65.6 39.4 %while.40 = (s32[]{:T(128)}, f32[8,8,9,4096]{3,2,1,0:T(8,128)}, f32[8,8,9,64]{3,2,1,0:T(8,128)S(1)}, s32[8,8,4096]{2,1,0:T(8,128)}, s32[]{:T(128)}) while((s32[]{:T(128)}, f32[8,8,9,4096]{3,2,1,0:T(8,128)}, f32[8,8,9,64]{3,2,1,0:T(8,128)S(1)}, s32[8,8,4096]{2,1,0:T(8,128)}, s32[]{:T(128)}) %tuple.115), condition=%wide.region_3.0_spmd, body=%wide.region_2.0_spmd.sunk | while | flops 228589568 | bytes 2556993 | solution.py:61
  104.9 14.9 %copy.26 = f32[64,9,4096]{2,0,1:T(8,128)} copy(f32[64,9,4096]{2,1,0:T(8,128)} %bitcast.161) | data formatting | bytes 18874368 | tf_op jit(solution)/shard_map/mul | solution.py:72
  119.8 8.0 %fusion.22 = f32[64,2,4096]{2,0,1:T(8,128)S(1)} fusion(bf16[64,2,9,4096]{3,0,2,1:T(8,128)(2,1)} %bitcast.152, f32[64,9,4096]{2,0,1:T(8,128)} %copy.26), kind=kLoop, calls=%fused_computation.40 | loop fusion | flops 13631488 | bytes 20971520 | tf_op jit(solution)/shard_map/reduce_sum | solution.py:72
  132.5 69.4 %all-reduce.13.cloned.1.call-done = (f32[6,65536]{1,0:T(8,128)}, f32[3,65536]{1,0:T(4,128)}) async-done(((f32[6,65536]{1,0:T(8,128)}, f32[3,65536]{1,0:T(4,128)}), (f32[6,65536]{1,0:T(8,128)}, f32[3,65536]{1,0:T(4,128)})) %all-reduce.13.cloned.1.call-update) | async-done | bytes 2359312 | tf_op jit(solution)/shard_map/psum | solution.py:128
  201.9 6.8 fusion.84
  211.5 6.5 stack.79
  235.7 11.2 %fusion.23 = f32[64,9,4096]{2,0,1:T(8,128)} fusion(bf16[64,2,9,4096]{3,0,2,1:T(8,128)(2,1)} %bitcast.153, f32[64,2,4096]{2,0,1:T(8,128)} %sub.44), kind=kLoop, calls=%fused_computation.41 | loop fusion | flops 11796480 | bytes 20971520 | tf_op jit(solution)/shard_map/reduce_sum | solution.py:144
  247.7 58.1 %while.41 = (s32[]{:T(128)}, f32[8,8,9,64]{3,2,1,0:T(8,128)}, f32[8,8,9,4096]{3,1,0,2:T(8,128)}, s32[8,8,4096]{2,1,0:T(8,128)}, s32[]{:T(128)}) while((s32[]{:T(128)}, f32[8,8,9,64]{3,2,1,0:T(8,128)}, f32[8,8,9,4096]{3,1,0,2:T(8,128)}, s32[8,8,4096]{2,1,0:T(8,128)}, s32[]{:T(128)}) %tuple.111), condition=%wide.region_17.18_spmd, body=%wide.region_16.17_spmd.sunk | while | flops 228589568 | bytes 3998277 | solution.py:85
  250.2 5.0 fusion.96
  257.4 5.0 fusion.96
  264.7 5.0 fusion.96
  271.9 5.0 fusion.96
  279.2 5.0 fusion.96
  286.4 5.0 fusion.96
  293.7 5.0 fusion.96
  300.9 5.0 fusion.96
  313.7 36.7 %all_gather.7 = f32[9,16384]{1,0:T(8,128)} all-gather(f32[9,2048]{1,0:T(8,128)S(1)} %copy-done.12), channel_id=1, replica_groups=mesh['cam'=4,'pt'=8] {'pt'}, dimensions={1}, use_global_device_ids=true | all-gather | bytes 663552 | tf_op jit(solution)/shard_map/all_gather | solution.py:131
  350.4 49.2 %all-reduce.7.cloned.1.call-done = f32[9,16384]{1,0:T(8,128)} async-done(((f32[9,16384]{1,0:T(8,128)}), f32[9,16384]{1,0:T(8,128)}) %all-reduce.7.cloned.1.call-update) | async-done | bytes 589840 | tf_op jit(solution)/shard_map/psum | solution.py:151
  402.3 7.1 all-reduce
  414.5 6.6 psum.68
  434.1 7.8 %broadcast.107 = f32[8,8,9,4096]{3,2,1,0:T(8,128)} broadcast(f32[]{:T(128)} %constant.49.clone.1), dimensions={} | broadcast | bytes 9437188 | tf_op jit(solution)/shard_map/broadcast.5
  441.9 45.9 %while.42 = (s32[]{:T(128)}, f32[8,8,9,4096]{3,2,1,0:T(8,128)}, f32[8,8,9,64]{3,2,1,0:T(8,128)}, s32[8,8,4096]{2,1,0:T(8,128)}, s32[]{:T(128)}) while((s32[]{:T(128)}, f32[8,8,9,4096]{3,2,1,0:T(8,128)}, f32[8,8,9,64]{3,2,1,0:T(8,128)}, s32[8,8,4096]{2,1,0:T(8,128)}, s32[]{:T(128)}) %tuple.114), condition=%wide.region_24.25_spmd, body=%wide.region_23.24_spmd.sunk | while | flops 228589568 | bytes 2556993 | solution.py:61
  487.8 14.9 %copy.31 = f32[64,9,4096]{2,0,1:T(8,128)} copy(f32[64,9,4096]{2,1,0:T(8,128)} %bitcast.162) | data formatting | bytes 18874368 | tf_op jit(solution)/shard_map/mul | solution.py:72
  502.6 7.6 %fusion.24 = f32[64,2,4096]{2,0,1:T(8,128)S(1)} fusion(bf16[64,2,9,4096]{3,0,2,1:T(8,128)(2,1)} %bitcast.154, f32[64,9,4096]{2,0,1:T(8,128)} %copy.31), kind=kLoop, calls=%fused_computation.42 | loop fusion | flops 13631488 | bytes 20971520 | tf_op jit(solution)/shard_map/reduce_sum | solution.py:72
  514.9 35.6 %all-reduce.9.cloned.1.call-done = f32[3,65536]{1,0:T(4,128)} async-done(((f32[3,65536]{1,0:T(4,128)}), f32[3,65536]{1,0:T(4,128)}) %all-reduce.9.cloned.1.call-update) | async-done | bytes 786448 | tf_op jit(solution)/shard_map/psum | solution.py:139
  550.5 11.2 %add_reduce_fusion.2 = (f32[65536]{0:T(1024)}, f32[65536]{0:T(1024)}, f32[65536]{0:T(1024)S(1)}) fusion(f32[6,65536]{1,0:T(8,128)} %copy-done.7, f32[3,65536]{1,0:T(4,128)} %all-reduce.9.cloned.1.call-done), kind=kLoop, calls=%fused_computation.102 | loop fusion | flops 983040 | bytes 3145728 | tf_op jit(solution)/shard_map/add | solution.py:45
  570.2 10.6 %fusion.25 = f32[64,9,4096]{2,0,1:T(8,128)} fusion(bf16[64,2,9,4096]{3,0,2,1:T(8,128)(2,1)} %bitcast.155, f32[64,2,4096]{2,0,1:T(8,128)S(1)} %sub.46), kind=kLoop, calls=%fused_computation.43 | loop fusion | flops 11796480 | bytes 20971520 | tf_op jit(solution)/shard_map/reduce_sum | solution.py:144
  580.9 53.1 %while.43 = (s32[]{:T(128)}, f32[8,8,9,64]{3,2,1,0:T(8,128)S(1)}, f32[8,8,9,4096]{3,1,0,2:T(8,128)}, s32[8,8,4096]{2,1,0:T(8,128)}, s32[]{:T(128)}) while((s32[]{:T(128)}, f32[8,8,9,64]{3,2,1,0:T(8,128)S(1)}, f32[8,8,9,4096]{3,1,0,2:T(8,128)}, s32[8,8,4096]{2,1,0:T(8,128)}, s32[]{:T(128)}) %tuple.113), condition=%wide.region_31.32_spmd, body=%wide.region_30.31_spmd.sunk | while | flops 228589568 | bytes 3997769 | solution.py:85
  638.8 79.0 %all-reduce.11.cloned.1.call-done = f32[9,16384]{1,0:T(8,128)} async-done(((f32[9,16384]{1,0:T(8,128)}), f32[9,16384]{1,0:T(8,128)}) %all-reduce.11.cloned.1.call-update) | async-done | bytes 589840 | tf_op jit(solution)/shard_map/psum | solution.py:151
  719.9 7.1 psum.71
  (165 shorter events, 245.1 us)
Async XLA Ops:
  7.2 194.7 %all-reduce.13.cloned.1.call-start = ((), (), s32[]{:S(2)}) async-start(), calls=%async_computation.3 | async-start | bytes 6291456 | tf_op jit(solution)/shard_map/psum | solution.py:128
  11.9 0.7 copy-start.13
  16.0 2.3 copy-start.11
  18.2 37.3 %copy-start.14 = (s32[1,1,64]{2,1,0:T(1,128)S(1)}, s32[1,1,64]{2,1,0:T(1,128)}, u32[]{:S(2)}) copy-start(s32[1,1,64]{2,1,0:T(1,128)} %param.20) | copy-start | bytes 772
  53.0 4.8 copy-start.1
  119.8 8.0 %copy-start = (bf16[1,1,64,6,4096]{4,2,3,1,0:T(8,128)(2,1)S(1)}, bf16[1,1,64,6,4096]{4,2,3,1,0:T(8,128)(2,1)}, u32[]{:S(2)}) copy-start(bf16[1,1,64,6,4096]{4,2,3,1,0:T(8,128)(2,1)} %param.24) | copy-start | bytes 9437188
  127.8 1.4 copy-start.2
  132.5 267.1 %all-reduce.7.cloned.1.call-start = ((), (), s32[]{:S(2)}) async-start(), calls=%async_computation | async-start | bytes 2097152 | tf_op jit(solution)/shard_map/psum | solution.py:151
  201.9 8.7 %copy-start.9 = (f32[65536]{0:T(1024)S(1)}, f32[65536]{0:T(1024)}, u32[]{:S(2)}) copy-start(f32[65536]{0:T(1024)} %param.19) | copy-start | bytes 786436
  218.0 3.3 copy-start.10
  220.0 1.3 copy-start.7
  232.6 1.6 copy-start.3
  308.4 5.3 copy-start.12
  313.6 236.8 %all-reduce.9.cloned.1.call-start = ((), (), s32[]{:S(2)}) async-start(), calls=%async_computation.1 | async-start | bytes 2097152 | tf_op jit(solution)/shard_map/psum | solution.py:139
  510.2 1.4 copy-start.4
  514.9 202.9 %all-reduce.11.cloned.1.call-start = ((), (), s32[]{:S(2)}) async-start(), calls=%async_computation.2 | async-start | bytes 2097152 | tf_op jit(solution)/shard_map/psum | solution.py:151
  568.4 1.6 copy-start.5
  634.2 83.6 %copy-start.6 = (f32[9,16384]{1,0:T(8,128)S(1)}, f32[9,16384]{1,0:T(8,128)}, u32[]{:S(2)}) copy-start(f32[9,16384]{1,0:T(8,128)} %all_gather.7) | copy-start | bytes 1769476
  634.2 83.6 %copy-start.8 = (f32[9,16384]{1,0:T(8,128)S(1)}, f32[9,16384]{1,0:T(8,128)}, u32[]{:S(2)}) copy-start(f32[9,16384]{1,0:T(8,128)} %multiply_add_fusion.1) | copy-start | bytes 1769476
Sparse Core Ops, SparseCore 0:
  132.6 69.2 all-reduce.12
  313.8 85.7 all-reduce.6
  515.0 35.4 all-reduce.8
  638.9 78.8 all-reduce.10
where the time goes:
time: 747 us; the launch traced here: 737 us
  waiting for transfers between devices  233 us (31%)
  matrix products  159 us (21%)
  local copies, waits for them, and re-layouts  153 us (20%)
  blocking collectives  92.2 us (12%)
  other arithmetic  79.7 us (11%)
  between operations  19.2 us (3%)
    psum x2, waiting for transfers between devices, per_device(): lax.psum(group_sum.reshape(9, blk_group * BLOCK), 'pt')  128 us
    dot_general x16, matrix products, camera_per_group(): return jnp.einsum('gkn,gnb->gkb', pushed_group, one_hot, precision=HIGH)  74.6 us
    dot_general x16, matrix products, select_per_group(): return jnp.einsum('gkb,gnb->gkn', picked_group, one_hot, precision=HIGH)  70.4 us
    psum x1, waiting for transfers between devices, per_device(): inverse = invert_points(lax.psum(hess_local, 'cam'), point_damping)  69.4 us
    all_gather x1, blocking collectives, per_device(): lax.all_gather(cam_damping, 'pt', axis=1, tiled=True)  36.7 us
    psum x1, waiting for transfers between devices, per_device(): lax.psum(collect(selector, pulled), 'cam')  35.6 us
    all_gather x1, blocking collectives, per_device(): lax.all_gather(right_side, 'pt', axis=1, tiled=True)  34.7 us
    mul x2, local copies, waits for them, and re-layouts, project(): return jnp.sum(cam_jac * at_camera[:, None], axis=2)  29.7 us
  transfers between devices with their start and end apart: 4, of which 4 were waited for; matrix products, arithmetic and copies ran while one was open for 0% of the time, Pallas kernels for 0%

commit v1 on v0

--- a/solution.py
+++ b/solution.py
@@ -148,7 +148,9 @@
             camera_sums(pushed, index_here) * live_pairs[:, None, None],
             precision=HIGH,
         )
-        image = damping_here * direction + lax.psum(group_sum.reshape(9, blk_group * BLOCK), "pt")
+        image = damping_here * direction + jnp.sum(
+            lax.all_gather(group_sum.reshape(9, blk_group * BLOCK), "pt"), axis=0
+        )
         step_size = norm_now / dot_whole(direction, image)
         solution = solution + step_size * direction
         residual = residual - step_size * image

time: 747 us -> 843 us (1.13)
  waiting for transfers between devices: 233 us -> 321 us
  other arithmetic: 79.7 us -> 88.6 us
    all_gather x0 -> x2, waiting for transfers between devices: none -> 217 us  [per_device(): lax.all_gather(group_sum.reshape(9, blk_group * BLOCK), 'pt')]
    psum x2 -> x0, waiting for transfers between devices: 128 us -> none  [per_device(): lax.psum(group_sum.reshape(9, blk_group * BLOCK), 'pt')]
    reduce_sum x0 -> x2, other arithmetic: none -> 8.96 us  [per_device(): jnp.sum(lax.all_gather(group_sum.reshape(9, blk_group * BLOCK), 'pt'), ax...]
    another operation x4 -> x6, local copies, waits for them, and re-layouts: 16.5 us -> 20.7 us
where the time goes in v1:
time: 843 us; the launch traced here: 833 us
  waiting for transfers between devices  321 us (38%)
  matrix products  159 us (19%)
  local copies, waits for them, and re-layouts  151 us (18%)
  blocking collectives  93.4 us (11%)
  other arithmetic  88.6 us (11%)
  between operations  19 us (2%)
    all_gather x2, waiting for transfers between devices, per_device(): lax.all_gather(group_sum.reshape(9, blk_group * BLOCK), 'pt')  217 us
    dot_general x16, matrix products, camera_per_group(): return jnp.einsum('gkn,gnb->gkb', pushed_group, one_hot, precision=HIGH)  74.6 us
    dot_general x16, matrix products, select_per_group(): return jnp.einsum('gkb,gnb->gkn', picked_group, one_hot, precision=HIGH)  70.4 us
    psum x1, waiting for transfers between devices, per_device(): inverse = invert_points(lax.psum(hess_local, 'cam'), point_damping)  69.4 us
    all_gather x1, blocking collectives, per_device(): lax.all_gather(cam_damping, 'pt', axis=1, tiled=True)  38.6 us
    all_gather x1, blocking collectives, per_device(): lax.all_gather(right_side, 'pt', axis=1, tiled=True)  34.7 us
    psum x1, waiting for transfers between devices, per_device(): lax.psum(collect(selector, pulled), 'cam')  34.1 us
    mul x2, local copies, waits for them, and re-layouts, project(): return jnp.sum(cam_jac * at_camera[:, None], axis=2)  29.7 us
  transfers between devices with their start and end apart: 4, of which 4 were waited for; matrix products, arithmetic and copies ran while one was open for 0% of the time, Pallas kernels for 0%

profile of v1, /device:TPU:0, one launch (start us, length us, event | category | flops | bytes accessed | tf_op | source)
XLA Modules:
  0.0 832.9 jit_solution(9699115200828610479)
XLA Ops:
  18.2 34.7 %all_gather.12 = f32[9,16384]{1,0:T(8,128)S(1)} all-gather(f32[9,2048]{1,0:T(8,128)S(1)} %copy-done.11), channel_id=1, replica_groups=mesh['cam'=4,'pt'=8] {'pt'}, dimensions={1}, use_global_device_ids=true | all-gather | bytes 663552 | tf_op jit(solution)/shard_map/all_gather | solution.py:130
  57.7 7.8 broadcast.107.clone
  65.6 39.4 %while.40 = (s32[]{:T(128)}, f32[8,8,9,4096]{3,2,1,0:T(8,128)}, f32[8,8,9,64]{3,2,1,0:T(8,128)S(1)}, s32[8,8,4096]{2,1,0:T(8,128)}, s32[]{:T(128)}) while((s32[]{:T(128)}, f32[8,8,9,4096]{3,2,1,0:T(8,128)}, f32[8,8,9,64]{3,2,1,0:T(8,128)S(1)}, s32[8,8,4096]{2,1,0:T(8,128)}, s32[]{:T(128)}) %tuple.115), condition=%wide.region_3.0_spmd, body=%wide.region_2.0_spmd.sunk | while | flops 228589568 | bytes 2556993 | solution.py:61
  105.0 14.9 %copy.26 = f32[64,9,4096]{2,0,1:T(8,128)} copy(f32[64,9,4096]{2,1,0:T(8,128)} %bitcast.161) | data formatting | bytes 18874368 | tf_op jit(solution)/shard_map/mul | solution.py:72
  119.9 8.1 fusion.22
  132.7 69.4 %all-reduce.7.cloned.1.call-done = (f32[6,65536]{1,0:T(8,128)}, f32[3,65536]{1,0:T(4,128)}) async-done(((f32[6,65536]{1,0:T(8,128)}, f32[3,65536]{1,0:T(4,128)}), (f32[6,65536]{1,0:T(8,128)}, f32[3,65536]{1,0:T(4,128)})) %all-reduce.7.cloned.1.call-update) | async-done | bytes 2359312 | tf_op jit(solution)/shard_map/psum | solution.py:128
  202.0 6.8 fusion.84
  211.7 6.6 stack.79
  236.0 11.2 %fusion.23 = f32[64,9,4096]{2,0,1:T(8,128)} fusion(bf16[64,2,9,4096]{3,0,2,1:T(8,128)(2,1)} %bitcast.153, f32[64,2,4096]{2,0,1:T(8,128)} %sub.44), kind=kLoop, calls=%fused_computation.41 | loop fusion | flops 11796480 | bytes 20971520 | tf_op jit(solution)/shard_map/reduce_sum | solution.py:144
  248.0 58.1 %while.41 = (s32[]{:T(128)}, f32[8,8,9,64]{3,2,1,0:T(8,128)}, f32[8,8,9,4096]{3,1,0,2:T(8,128)}, s32[8,8,4096]{2,1,0:T(8,128)}, s32[]{:T(128)}) while((s32[]{:T(128)}, f32[8,8,9,64]{3,2,1,0:T(8,128)}, f32[8,8,9,4096]{3,1,0,2:T(8,128)}, s32[8,8,4096]{2,1,0:T(8,128)}, s32[]{:T(128)}) %tuple.111), condition=%wide.region_17.18_spmd, body=%wide.region_16.17_spmd.sunk | while | flops 228589568 | bytes 3998277 | solution.py:85
  250.5 5.0 fusion.96
  257.7 5.0 fusion.96
  265.0 5.0 fusion.96
  272.2 5.0 fusion.96
  279.4 5.0 fusion.96
  286.7 5.0 fusion.96
  293.9 5.0 fusion.96
  301.2 5.0 fusion.96
  314.0 38.6 %all_gather.13 = f32[9,16384]{1,0:T(8,128)} all-gather(f32[9,2048]{1,0:T(8,128)S(1)} %copy-done.12), channel_id=1, replica_groups=mesh['cam'=4,'pt'=8] {'pt'}, dimensions={1}, use_global_device_ids=true | all-gather | bytes 663552 | tf_op jit(solution)/shard_map/all_gather | solution.py:131
  352.6 92.4 %all-gather.3.cloned.1.call-done = f32[8,9,16384]{2,1,0:T(8,128)} async-done(((f32[1,9,16384]{2,1,0:T(8,128)}), f32[8,9,16384]{2,1,0:T(8,128)}) %all-gather.3.cloned.1.call-update) | async-done | bytes 4718608 | tf_op jit(solution)/shard_map/all_gather | solution.py:152
  452.7 6.5 all-reduce
  464.1 7.2 psum.53
  484.4 7.8 broadcast.107
  492.2 45.9 %while.42 = (s32[]{:T(128)}, f32[8,8,9,4096]{3,2,1,0:T(8,128)}, f32[8,8,9,64]{3,2,1,0:T(8,128)}, s32[8,8,4096]{2,1,0:T(8,128)}, s32[]{:T(128)}) while((s32[]{:T(128)}, f32[8,8,9,4096]{3,2,1,0:T(8,128)}, f32[8,8,9,64]{3,2,1,0:T(8,128)}, s32[8,8,4096]{2,1,0:T(8,128)}, s32[]{:T(128)}) %tuple.114), condition=%wide.region_24.25_spmd, body=%wide.region_23.24_spmd.sunk | while | flops 228589568 | bytes 2556993 | solution.py:61
  538.1 14.9 %copy.31 = f32[64,9,4096]{2,0,1:T(8,128)} copy(f32[64,9,4096]{2,1,0:T(8,128)} %bitcast.162) | data formatting | bytes 18874368 | tf_op jit(solution)/shard_map/mul | solution.py:72
  552.9 8.0 fusion.24
  565.6 34.1 %all-reduce.5.cloned.1.call-done = f32[3,65536]{1,0:T(4,128)} async-done(((f32[3,65536]{1,0:T(4,128)}), f32[3,65536]{1,0:T(4,128)}) %all-reduce.5.cloned.1.call-update) | async-done | bytes 786448 | tf_op jit(solution)/shard_map/psum | solution.py:139
  599.7 10.9 %add_reduce_fusion.2 = (f32[65536]{0:T(1024)}, f32[65536]{0:T(1024)}, f32[65536]{0:T(1024)S(1)}) fusion(f32[6,65536]{1,0:T(8,128)} %copy-done.7, f32[3,65536]{1,0:T(4,128)} %all-reduce.5.cloned.1.call-done), kind=kLoop, calls=%fused_computation.102 | loop fusion | flops 983040 | bytes 3145728 | tf_op jit(solution)/shard_map/add | solution.py:45
  619.2 10.6 %fusion.25 = f32[64,9,4096]{2,0,1:T(8,128)} fusion(bf16[64,2,9,4096]{3,0,2,1:T(8,128)(2,1)} %bitcast.155, f32[64,2,4096]{2,0,1:T(8,128)S(1)} %sub.46), kind=kLoop, calls=%fused_computation.43 | loop fusion | flops 11796480 | bytes 20971520 | tf_op jit(solution)/shard_map/reduce_sum | solution.py:144
  629.9 53.2 %while.43 = (s32[]{:T(128)}, f32[8,8,9,64]{3,2,1,0:T(8,128)S(1)}, f32[8,8,9,4096]{3,1,0,2:T(8,128)}, s32[8,8,4096]{2,1,0:T(8,128)}, s32[]{:T(128)}) while((s32[]{:T(128)}, f32[8,8,9,64]{3,2,1,0:T(8,128)S(1)}, f32[8,8,9,4096]{3,1,0,2:T(8,128)}, s32[8,8,4096]{2,1,0:T(8,128)}, s32[]{:T(128)}) %tuple.113), condition=%wide.region_31.32_spmd, body=%wide.region_30.31_spmd.sunk | while | flops 228589568 | bytes 3997769 | solution.py:85
  685.6 125.1 %all-gather.5.cloned.1.call-done = f32[8,9,16384]{2,1,0:T(8,128)} async-done(((f32[1,9,16384]{2,1,0:T(8,128)}), f32[8,9,16384]{2,1,0:T(8,128)}) %all-gather.5.cloned.1.call-update) | async-done | bytes 4718608 | tf_op jit(solution)/shard_map/all_gather | solution.py:152
  816.6 6.4 psum.55
  (167 shorter events, 251.5 us)
Async XLA Ops:
  7.2 194.9 %all-reduce.7.cloned.1.call-start = ((), (), s32[]{:S(2)}) async-start(), calls=%async_computation.3 | async-start | bytes 6291456 | tf_op jit(solution)/shard_map/psum | solution.py:128
  11.9 0.7 copy-start.13
  16.0 2.3 copy-start.11
  18.2 37.3 %copy-start.14 = (s32[1,1,64]{2,1,0:T(1,128)S(1)}, s32[1,1,64]{2,1,0:T(1,128)}, u32[]{:S(2)}) copy-start(s32[1,1,64]{2,1,0:T(1,128)} %param.20) | copy-start | bytes 772
  53.0 4.8 copy-start.1
  119.9 8.1 copy-start
  127.9 1.4 copy-start.2
  132.6 312.4 %all-gather.3.cloned.1.call-start = ((), (), s32[]{:S(2)}) async-start(), calls=%async_computation | async-start | bytes 9437184 | tf_op jit(solution)/shard_map/all_gather | solution.py:152
  202.0 8.7 %copy-start.9 = (f32[65536]{0:T(1024)S(1)}, f32[65536]{0:T(1024)}, u32[]{:S(2)}) copy-start(f32[65536]{0:T(1024)} %param.19) | copy-start | bytes 786436
  218.3 3.3 copy-start.10
  220.3 1.3 copy-start.7
  232.9 1.6 copy-start.3
  308.7 5.3 copy-start.12
  313.9 285.7 %all-reduce.5.cloned.1.call-start = ((), (), s32[]{:S(2)}) async-start(), calls=%async_computation.1 | async-start | bytes 2097152 | tf_op jit(solution)/shard_map/psum | solution.py:139
  560.9 1.4 copy-start.4
  565.6 245.2 %all-gather.5.cloned.1.call-start = ((), (), s32[]{:S(2)}) async-start(), calls=%async_computation.2 | async-start | bytes 9437184 | tf_op jit(solution)/shard_map/all_gather | solution.py:152
  617.4 1.6 copy-start.5
  685.6 129.1 %copy-start.6 = (f32[9,16384]{1,0:T(8,128)S(1)}, f32[9,16384]{1,0:T(8,128)}, u32[]{:S(2)}) copy-start(f32[9,16384]{1,0:T(8,128)} %all_gather.13) | copy-start | bytes 1769476
  685.6 129.1 %copy-start.8 = (f32[9,16384]{1,0:T(8,128)S(1)}, f32[9,16384]{1,0:T(8,128)}, u32[]{:S(2)}) copy-start(f32[9,16384]{1,0:T(8,128)} %multiply_add_fusion.1) | copy-start | bytes 1769476
Sparse Core Ops, SparseCore 0:
  132.7 69.2 all-reduce.6
  314.1 130.8 all-gather.2
  565.7 33.9 all-reduce.4
  685.7 124.9 all-gather.4
